TPU v7x, 32 devices: a whole 2x2x4 slice. The times are simulated.
32 devices in a mesh: groups: 2 (over y), dom: 4 (over z), sub: 4 (over x, core).
Axes of the slice: x: 2, y: 2, z: 4, core: 2. Of those that a mesh axis runs over, the one named last changes fastest.
Arguments:
- positions: float32 [3, 16, 16, 128], P(None, ('groups', 'dom'), 'sub'), parts along dimension 1, may hold values from -50 to 80, as said below
- charge: float32 [16, 16, 128], P(('groups', 'dom'), 'sub'), parts along dimension 0, may hold values from -2.5 to 2.5
- radius: float32 [16, 16, 128], P(('groups', 'dom'), 'sub'), parts along dimension 0, may hold values from 1.3 to 2.2
- segment: int32 [16, 16, 128], P(('groups', 'dom'), 'sub'), parts along dimension 0, may hold values from 0 to 15, never falling along the last dimension, each value on 1 to 16 neighbouring positions
- near_tiles: int32 [16, 16, 8], P(('groups', 'dom'), 'sub'), parts along dimension 0, may hold values from 0 to 1, as said below
Outputs:
- born_radii: float32 [16, 16, 128], P(('groups', 'dom'), 'sub'), parts along dimension 0
- radius_grad: float32 [16, 16, 128], P(('groups', 'dom'), 'sub'), parts along dimension 0
- forces: float32 [3, 16, 16, 128], P(None, ('groups', 'dom'), 'sub'), parts along dimension 1
There are 2 independent parts, one for each index of `groups`. A program takes and returns all parts, laid end to end along the dimension named above; each array names one. Nothing has to cross between parts.
Inputs may be any that keep to these rules, and one draw needn't show every extreme that they name: `positions`: coordinates in angstroms; the third runs along the fiber. near_tiles[a, b, k] is 1 when the partner tile of step k is near tile (a, b), else 0. The relation is symmetric: a tile is near its partner exactly when the partner is near it by the opposite step. No tile is near a tile beyond either end of the first tile dimension; the second dimension closes around the fiber. `segment`: within each tile the component numbers never fall along the atoms, and each of the 16 components has 1 to 16 atoms.
All inputs are finite; a program needn't handle non-finite values.
Results may differ from a plain program's by a relative error of at most 0.0003.
Values sent between devices are 32-bit elements; how exact they have to be, the bound alone decides.
No kernel may reach another device: no remote copies, remote signals or barrier semaphores. Data moves between devices by JAX's collectives and lax.ppermute only.
A program may use at most 64 MiB of HBM per device.

v0:
```python
import jax
import jax.numpy as jnp
from jax import lax
from jax.sharding import PartitionSpec as P

CT = 16
neighbour_steps = ((-1, -1), (-1, 0), (-1, 1), (0, -1), (0, 1), (1, -1), (1, 0), (1, 1))
switch_span = 64.0
radius_factor = 1.5
highest = lax.Precision.HIGHEST
far_block = 1024


def passed_along(shard, axis, by):
    size = lax.axis_size(axis)
    return lax.ppermute(shard, axis, [(i, (i + by) % size) for i in range(size)])


def extended(cells, sides, width):
    for axis, dim in sides:
        count = lax.axis_size(axis)
        head = lax.slice_in_dim(cells, 0, width, axis=dim)
        tail = lax.slice_in_dim(cells, cells.shape[dim] - width, cells.shape[dim], axis=dim)
        cells = jnp.concatenate(
            [
                lax.ppermute(tail, axis, [(i, (i + 1) % count) for i in range(count)]),
                cells,
                lax.ppermute(head, axis, [((i + 1) % count, i) for i in range(count)]),
            ],
            axis=dim,
        )
    return cells


def far_keep(tile_along, tile_round, tile_near, comp_along, comp_round, around_count):
    struck = (tile_along[:, None] == comp_along[None, :]) & (
        tile_round[:, None] == comp_round[None, :]
    )
    for slot_index, (step_z, step_s) in enumerate(neighbour_steps):
        flagged = (tile_near[:, slot_index] == 1)[:, None]
        same_along = (tile_along + step_z)[:, None] == comp_along[None, :]
        same_round = jnp.mod(tile_round + step_s, around_count)[:, None] == comp_round[None, :]
        struck = struck | flagged & same_along & same_round
    return jnp.logical_not(struck)


def pair_distance(own_pos, part_pos):
    dist_sq = jnp.zeros(own_pos.shape[1:] + (part_pos.shape[-1],), own_pos.dtype)
    for axis_slot in range(3):
        apart_axis = own_pos[axis_slot][..., :, None] - part_pos[axis_slot][..., None, :]
        dist_sq = dist_sq + apart_axis * apart_axis
    return dist_sq


def born_distance(dist_sq, product):
    return jnp.sqrt(dist_sq + product * jnp.exp(-dist_sq / (4.0 * product)))


def tile_screen(own_pos, part_pos, part_rho, keep_mask):
    dist_sq = pair_distance(own_pos, part_pos)
    radius_sq = part_rho[..., None, :] * part_rho[..., None, :]
    denom_sq = dist_sq + radius_sq
    pair_term = radius_sq * part_rho[..., None, :] / (denom_sq * denom_sq)
    return jnp.sum(jnp.where(keep_mask, pair_term, 0.0), axis=-1)


def tile_energy(own_pos, own_born, part_pos, part_q, part_born, keep_mask):
    dist_sq = pair_distance(own_pos, part_pos)
    product = own_born[..., :, None] * part_born[..., None, :]
    pair_term = part_q[..., None, :] / born_distance(dist_sq, product)
    return jnp.sum(jnp.where(keep_mask, pair_term, 0.0), axis=-1)


def centre_distance(flat_pos, centre):
    dist_sq = jnp.zeros((flat_pos.shape[1], centre.shape[1]), flat_pos.dtype)
    for axis_slot in range(3):
        apart_axis = flat_pos[axis_slot][:, None] - centre[axis_slot][None, :]
        dist_sq = dist_sq + apart_axis * apart_axis
    return dist_sq


def screen_block(flat_pos, centre, volume, comp_radius, keep):
    dist_sq = centre_distance(flat_pos, centre)
    weight = dist_sq / (dist_sq + switch_span)
    denom_sq = dist_sq + comp_radius * comp_radius
    return jnp.sum(jnp.where(keep, volume * weight / (denom_sq * denom_sq), 0.0), axis=1)


def potential_block(flat_pos, flat_born, centre, total_q, comp_radius, keep):
    dist_sq = centre_distance(flat_pos, centre)
    weight = dist_sq / (dist_sq + switch_span)
    product = flat_born[:, None] * comp_radius[None, :]
    return jnp.sum(jnp.where(keep, total_q * weight / born_distance(dist_sq, product), 0.0), axis=1)


def block_split(values, block_size):
    shaped = values.reshape(values.shape[:-1] + (values.shape[-1] // block_size, block_size))
    return jnp.moveaxis(shaped, -2, 0)


def far_screening(flat_pos, centre, volume, comp_radius, comp_along, comp_round, keep_fn):
    block_size = min(centre.shape[1], far_block)

    def accumulate(running, pieces):
        keep = keep_fn(pieces[3], pieces[4])
        return (running + screen_block(flat_pos, pieces[0], pieces[1], pieces[2], keep), None)

    inputs = (
        block_split(centre, block_size),
        block_split(volume, block_size),
        block_split(comp_radius, block_size),
        block_split(comp_along, block_size),
        block_split(comp_round, block_size),
    )
    return lax.scan(
        jax.checkpoint(accumulate), jnp.zeros((flat_pos.shape[1],), jnp.float32), inputs
    )[0]


def far_potential(
    flat_pos, flat_born, centre, total_q, comp_radius, comp_along, comp_round, keep_fn
):
    block_size = min(centre.shape[1], far_block)

    def accumulate(running, pieces):
        keep = keep_fn(pieces[3], pieces[4])
        return (
            running + potential_block(flat_pos, flat_born, pieces[0], pieces[1], pieces[2], keep),
            None,
        )

    inputs = (
        block_split(centre, block_size),
        block_split(total_q, block_size),
        block_split(comp_radius, block_size),
        block_split(comp_along, block_size),
        block_split(comp_round, block_size),
    )
    return lax.scan(
        jax.checkpoint(accumulate), jnp.zeros((flat_pos.shape[1],), jnp.float32), inputs
    )[0]


def components(positions, charge, radius, segment):
    onehot = (segment[..., None] == jnp.arange(CT, dtype=jnp.int32)).astype(jnp.float32)
    members = jnp.sum(onehot, axis=2)
    centre = jnp.einsum("kabl,ablc->kabc", positions, onehot, precision=highest) / members
    total_q = jnp.einsum("abl,ablc->abc", charge, onehot, precision=highest)
    volume = jnp.einsum("abl,ablc->abc", radius * radius * radius, onehot, precision=highest)
    comp_radius = (
        radius_factor * jnp.einsum("abl,ablc->abc", radius, onehot, precision=highest) / members
    )
    return (onehot, members, centre, total_q, volume, comp_radius)


def sub_pass(rim_piece, direction):
    return passed_along(rim_piece, "sub", direction)


def dom_pass(rim_piece, direction):
    return passed_along(rim_piece, "dom", direction)


def fold_rims(window_grad):
    tile_rows = window_grad.shape[1] - 2
    tile_cols = window_grad.shape[2] - 2
    inner_grid = window_grad[:, :, 1 : tile_cols + 1]
    inner_grid = inner_grid.at[:, :, tile_cols - 1].add(sub_pass(window_grad[:, :, 0], -1))
    inner_grid = inner_grid.at[:, :, 0].add(sub_pass(window_grad[:, :, tile_cols + 1], 1))
    own_grid = inner_grid[:, 1 : tile_rows + 1]
    own_grid = own_grid.at[:, tile_rows - 1].add(dom_pass(inner_grid[:, 0], -1))
    own_grid = own_grid.at[:, 0].add(dom_pass(inner_grid[:, tile_rows + 1], 1))
    return own_grid


def centre_spread(grad_table):
    partial_sums = lax.psum_scatter(grad_table, "dom", scatter_dimension=1, tiled=True)
    return lax.psum_scatter(partial_sums, "sub", scatter_dimension=1, tiled=True)


def local(positions, charge, radius, segment, near_tiles):
    tile_rows, tile_cols, tile_width = charge.shape
    sub_count = lax.axis_size("sub")
    around_count = tile_cols * sub_count
    self_keep = jnp.arange(tile_width)[:, None] != jnp.arange(tile_width)[None, :]
    atom_stack = jnp.concatenate([positions, charge[None], radius[None]], axis=0)
    window = extended(atom_stack, (("dom", 1), ("sub", 2)), 1)
    win_pos = window[0:3]
    win_q = window[3]
    win_rho = window[4]
    onehot, members, centre, total_q, volume, comp_radius = components(
        positions, charge, radius, segment
    )
    comp_table = jnp.concatenate(
        [
            centre.reshape(3, -1),
            total_q.reshape(1, -1),
            volume.reshape(1, -1),
            comp_radius.reshape(1, -1),
        ],
        axis=0,
    )
    sub_table = lax.all_gather(comp_table, "sub", axis=1, tiled=True)
    all_table = lax.all_gather(sub_table, "dom", axis=1, tiled=True)
    all_centre = all_table[0:3]
    all_charge = all_table[3]
    all_volume = all_table[4]
    all_radius = all_table[5]
    per_device = tile_rows * tile_cols * CT
    entry_index = jnp.arange(all_table.shape[1], dtype=jnp.int32)
    owner_device = entry_index // per_device
    local_entry = entry_index % per_device
    comp_along = owner_device // sub_count * tile_rows + local_entry // (tile_cols * CT)
    comp_round = owner_device % sub_count * tile_cols + local_entry // CT % tile_cols
    dom_index = lax.axis_index("dom")
    sub_index = lax.axis_index("sub")
    shape_three = (tile_rows, tile_cols, tile_width)
    along_grid = dom_index * tile_rows + jnp.arange(tile_rows, dtype=jnp.int32)[:, None, None]
    round_grid = sub_index * tile_cols + jnp.arange(tile_cols, dtype=jnp.int32)[None, :, None]
    tile_along = jnp.broadcast_to(along_grid, shape_three).reshape(-1)
    tile_round = jnp.broadcast_to(round_grid, shape_three).reshape(-1)
    tile_near = jnp.broadcast_to(near_tiles[:, :, None, :], shape_three + (8,)).reshape(-1, 8)

    def keep_fn(block_along, block_round):
        return far_keep(tile_along, tile_round, tile_near, block_along, block_round, around_count)

    def window_part(values, step_z, step_s):
        return values[
            ..., 1 + step_z : 1 + step_z + tile_rows, 1 + step_s : 1 + step_s + tile_cols, :
        ]

    def born_of(own_pos, near_pos, far_centre):
        screening = tile_screen(
            own_pos, window_part(near_pos, 0, 0), window_part(win_rho, 0, 0), self_keep
        )
        for slot_index, (step_z, step_s) in enumerate(neighbour_steps):
            keep_mask = (near_tiles[..., slot_index] == 1)[..., None, None]
            screening = screening + tile_screen(
                own_pos,
                window_part(near_pos, step_z, step_s),
                window_part(win_rho, step_z, step_s),
                keep_mask,
            )
        far_part = far_screening(
            own_pos.reshape(3, -1),
            far_centre,
            all_volume,
            all_radius,
            comp_along,
            comp_round,
            keep_fn,
        )
        screening = screening + far_part.reshape(screening.shape)
        return radius * (1.0 + radius * screening)

    born_radii, born_back = jax.vjp(born_of, positions, win_pos, all_centre)
    win_born = extended(born_radii, (("dom", 0), ("sub", 1)), 1)

    def energy_of(own_pos, own_born, near_pos, near_born, far_centre):
        potential = tile_energy(
            own_pos,
            own_born,
            window_part(near_pos, 0, 0),
            window_part(win_q, 0, 0),
            window_part(near_born, 0, 0),
            self_keep,
        )
        for slot_index, (step_z, step_s) in enumerate(neighbour_steps):
            keep_mask = (near_tiles[..., slot_index] == 1)[..., None, None]
            potential = potential + tile_energy(
                own_pos,
                own_born,
                window_part(near_pos, step_z, step_s),
                window_part(win_q, step_z, step_s),
                window_part(near_born, step_z, step_s),
                keep_mask,
            )
        far_part = far_potential(
            own_pos.reshape(3, -1),
            own_born.reshape(-1),
            far_centre,
            all_charge,
            all_radius,
            comp_along,
            comp_round,
            keep_fn,
        )
        potential = potential + far_part.reshape(potential.shape)
        return -0.5 * jnp.sum(charge * (charge / own_born + potential))

    energy_back = jax.vjp(energy_of, positions, born_radii, win_pos, win_born, all_centre)[1]
    grad_pos, grad_born, grad_window, grad_wborn, grad_centre = energy_back(
        jnp.ones((), jnp.float32)
    )
    radius_grad = grad_born + fold_rims(grad_wborn[None])[0]
    chain_pos, chain_window, chain_centre = born_back(radius_grad)
    own_centre = centre_spread(grad_centre + chain_centre)
    per_member = own_centre.reshape(centre.shape) / members
    centre_part = jnp.einsum("ablc,kabc->kabl", onehot, per_member, precision=highest)
    total_grad = grad_pos + chain_pos + fold_rims(grad_window + chain_window) + centre_part
    return (born_radii, radius_grad, -total_grad)


def solution(mesh):
    placed = (
        P(None, ("groups", "dom"), "sub", None),
        P(("groups", "dom"), "sub", None),
        P(("groups", "dom"), "sub", None),
        P(("groups", "dom"), "sub", None),
        P(("groups", "dom"), "sub", None),
    )
    return jax.shard_map(
        local,
        mesh=mesh,
        in_specs=placed,
        out_specs=(
            P(("groups", "dom"), "sub", None),
            P(("groups", "dom"), "sub", None),
            P(None, ("groups", "dom"), "sub", None),
        ),
        check_vma=False,
    )
```

profile of v0, /device:TPU:0, one launch (start us, length us, event | category | flops | bytes accessed | tf_op | source)
XLA Modules:
  0.0 267.3 jit_solution(454773463730050776)
XLA Ops:
  8.0 3.1 %collective-permute-start = (f32[5,1,4,128]{3,2,1,0:T(4,128)S(1)}, f32[5,1,4,128]{3,2,1,0:T(4,128)S(1)}, u32[]{:S(2)}, u32[]{:S(2)}) collective-permute-start(f32[5,1,4,128]{3,2,1,0:T(4,128)S(1)} %get-tuple-element.1764), channel_id=1, source_target_pairs={{0,4},{4,8},{8,12},{12,0},{1,5},{5,9},{9,13},{13,1},{2,6},{6,10},{... | collective-permute-start | bytes 30728 | tf_op jit(solution)/shard_map/ppermute | solution.py:26
  11.1 2.1 collective-permute-start.1
  20.8 5.2 %all_gather.6 = f32[6,512]{1,0:T(8,128)S(1)} all-gather(f32[6,128]{1,0:T(8,128)S(1)} %pad_maximum_fusion.40), channel_id=1, replica_groups=mesh['groups'=2,'dom'=4,'sub'=4] {'sub'}, dimensions={1}, use_global_device_ids=true | all-gather | bytes 15360 | tf_op jit(solution)/shard_map/all_gather | solution.py:203
  26.8 13.1 %all_gather.7 = f32[6,2048]{1,0:T(8,128)S(1)} all-gather(f32[6,512]{1,0:T(8,128)S(1)} %all_gather.6), channel_id=1, replica_groups=mesh['groups'=2,'dom'=4,'sub'=4] {'dom'}, dimensions={1}, use_global_device_ids=true | all-gather | bytes 61440 | tf_op jit(solution)/shard_map/all_gather | solution.py:204
  44.9 20.9 %while.65 = (s32[]{:T(128)}, f32[1024]{0:T(1024)S(1)}, s32[2,1024]{1,0:T(2,128)S(1)}, s32[2,1024]{1,0:T(2,128)S(1)}, pred[1024,1]{0,1:T(4,128)(4,1)S(1)}, /*inde...) while((s32[]{:T(128)}, f32[1024]{0:T(1024)S(1)}, ...), condition=%wide.region_12.13_spmd.clone.clone.clone, body=%wide.region_10.12_spmd.clone.clone.clone.sunk | while | flops 50371588 | bytes 205115 | solution.py:115
  45.4 10.0 %select_reduce_fusion.11 = f32[1024]{0:T(1024)S(1)} fusion(f32[1024]{0:T(1024)S(1)} %bitcast.622, f32[1024]{0:T(1024)S(1)} %bitcast.592, f32[1024]{0:T(1024)S(1)} %bitcast.691, f32[1024]{0:T(1024)S(1)} %bitcast.591, f32[1024]{0:T(1024)S(1)} %bitcast.695, f32[1024]{0:T(1024)S(1)} %bitcast.590, f32[1024]{0:T(1024)S(1)} %bitcast.693, ...), kind=kLoop, calls=%fused_computation.229.clone.1 | loop fusion | flops 50330624 | bytes 81920 | tf_op jit(solution)/shard_map/jvp()/while/body/eval_jaxpr/reduce_sum | solution.py:86
  55.8 10.0 %select_reduce_fusion.11 = f32[1024]{0:T(1024)S(1)} fusion(f32[1024]{0:T(1024)S(1)} %bitcast.622, f32[1024]{0:T(1024)S(1)} %bitcast.592, f32[1024]{0:T(1024)S(1)} %bitcast.691, f32[1024]{0:T(1024)S(1)} %bitcast.591, f32[1024]{0:T(1024)S(1)} %bitcast.695, f32[1024]{0:T(1024)S(1)} %bitcast.590, f32[1024]{0:T(1024)S(1)} %bitcast.693, ...), kind=kLoop, calls=%fused_computation.229.clone.1 | loop fusion | flops 50330624 | bytes 81920 | tf_op jit(solution)/shard_map/jvp()/while/body/eval_jaxpr/reduce_sum | solution.py:86
  70.1 3.7 %collective-permute-start.5 = (f32[1,4,128]{2,1,0:T(4,128)S(1)}, f32[1,4,128]{2,1,0:T(4,128)S(1)}, u32[]{:S(2)}, u32[]{:S(2)}) collective-permute-start(f32[1,4,128]{2,1,0:T(4,128)S(1)} %get-tuple-element.1814), channel_id=1, source_target_pairs={{4,0},{8,4},{12,8},{0,12},{5,1},{9,5},{13,9},{1,13},{6,2},{10,6},{... | collective-permute-start | bytes 6152 | tf_op jit(solution)/shard_map/ppermute | solution.py:28
  73.8 61.9 %while.63 = (s32[]{:T(128)}, f32[3,1024]{1,0:T(4,128)S(1)}, f32[1024]{0:T(1024)S(1)}, f32[1024]{0:T(1024)S(1)}, f32[2,3,1024]{2,1,0:T(4,128)S(1)}, /*index=5*/f3...) while((s32[]{:T(128)}, f32[3,1024]{1,0:T(4,128)S(1)}, ...), condition=%wide.region_21.22_spmd.clone, body=%wide.region_13.21_spmd.clone.sunk | while | flops 160494592 | bytes 520676 | solution.py:139
  74.3 14.4 %multiply_reduce_fusion.20 = f32[1024]{0:T(1024)S(1)} fusion(f32[1024]{0:T(1024)S(1)} %bitcast.599, f32[1024]{0:T(1024)S(1)} %get-tuple-element.2180, f32[1024]{0:T(1024)S(1)} %bitcast.606, f32[1024]{0:T(1024)S(1)} %bitcast.615, f32[1024]{0:T(1024)S(1)} %bitcast.608, f32[1024]{0:T(1024)S(1)} %bitcast.617, f32[1024]{0:T(1024)S(1)} %bitcast.604, ...), kind=kLoop, calls=%fused_computation.76.clone.1 | loop fusion | flops 72350720 | bytes 90112 | tf_op jit(solution)/shard_map/transpose(jvp())/while/body/eval_jaxpr/checkpoint/reduce_sum | solution.py:92
  88.7 15.9 %fusion.521 = (f32[1024]{0:T(1024)S(1)}, f32[1024]{0:T(1024)S(1)}, f32[1024]{0:T(1024)S(1)}, f32[1024]{0:T(1024)S(1)}, f32[1024]{0:T(1024)S(1)}, /*index=5*/f32[1024]{0:T(1024)S(1)}) fusion(f32[1024]{0:T(1024)S(1)} %bitcast.605, f32[1024]{0:T(1024)S(1)} %bitcast.614, f32[1024]{0:T(1024)S(1)} %bitcast.609, f32[1024]{0:T(1024)S(1)} %bitcast.618, ...), kind=kLoop, calls=%fused_computation.89.clone.1 | loop fusion | flops 88074240 | bytes 110592 | tf_op jit(solution)/shard_map/transpose(jvp())/while/body/eval_jaxpr/checkpoint/reduce_sum | solution.py:77
  105.2 14.4 %multiply_reduce_fusion.20 = f32[1024]{0:T(1024)S(1)} fusion(f32[1024]{0:T(1024)S(1)} %bitcast.599, f32[1024]{0:T(1024)S(1)} %get-tuple-element.2180, f32[1024]{0:T(1024)S(1)} %bitcast.606, f32[1024]{0:T(1024)S(1)} %bitcast.615, f32[1024]{0:T(1024)S(1)} %bitcast.608, f32[1024]{0:T(1024)S(1)} %bitcast.617, f32[1024]{0:T(1024)S(1)} %bitcast.604, ...), kind=kLoop, calls=%fused_computation.76.clone.1 | loop fusion | flops 72350720 | bytes 90112 | tf_op jit(solution)/shard_map/transpose(jvp())/while/body/eval_jaxpr/checkpoint/reduce_sum | solution.py:92
  119.6 15.9 %fusion.521 = (f32[1024]{0:T(1024)S(1)}, f32[1024]{0:T(1024)S(1)}, f32[1024]{0:T(1024)S(1)}, f32[1024]{0:T(1024)S(1)}, f32[1024]{0:T(1024)S(1)}, /*index=5*/f32[1024]{0:T(1024)S(1)}) fusion(f32[1024]{0:T(1024)S(1)} %bitcast.605, f32[1024]{0:T(1024)S(1)} %bitcast.614, f32[1024]{0:T(1024)S(1)} %bitcast.609, f32[1024]{0:T(1024)S(1)} %bitcast.618, ...), kind=kLoop, calls=%fused_computation.89.clone.1 | loop fusion | flops 88074240 | bytes 110592 | tf_op jit(solution)/shard_map/transpose(jvp())/while/body/eval_jaxpr/checkpoint/reduce_sum | solution.py:77
  138.8 3.7 %fusion.382 = (f32[2,4,128]{2,1,0:T(4,128)S(1)}, f32[2,4,128]{2,1,0:T(4,128)S(1)}, f32[2,4,128]{2,1,0:T(4,128)S(1)}, f32[2,4,128]{2,1,0:T(4,128)S(1)}, f32[2,4,1...) fusion(f32[2,4,128]{2,1,0:T(4,128)S(1)} %get-tuple-element.1743, ...), kind=kLoop, calls=%fused_computation.648 | loop fusion | flops 13352960 | bytes 126992 | tf_op jit(solution)/shard_map/transpose(jvp())/reduce_sum | solution.py:50
  142.7 3.7 %fusion.406 = (f32[2,4,128]{2,1,0:T(4,128)S(1)}, f32[2,4,128]{2,1,0:T(4,128)S(1)}, f32[2,4,128]{2,1,0:T(4,128)S(1)}, f32[2,4,128]{2,1,0:T(4,128)S(1)}, f32[2,4,1...) fusion(f32[2,4,128]{2,1,0:T(4,128)S(1)} %get-tuple-element.1739, ...), kind=kLoop, calls=%fused_computation.672 | loop fusion | flops 13352960 | bytes 126992 | tf_op jit(solution)/shard_map/transpose(jvp())/reduce_sum | solution.py:50
  146.6 3.7 %fusion.430 = (f32[2,4,128]{2,1,0:T(4,128)S(1)}, f32[2,4,128]{2,1,0:T(4,128)S(1)}, f32[2,4,128]{2,1,0:T(4,128)S(1)}, f32[2,4,128]{2,1,0:T(4,128)S(1)}, f32[2,4,1...) fusion(f32[2,4,128]{2,1,0:T(4,128)S(1)} %get-tuple-element.1759, ...), kind=kLoop, calls=%fused_computation.696 | loop fusion | flops 13352960 | bytes 126992 | tf_op jit(solution)/shard_map/transpose(jvp())/reduce_sum | solution.py:50
  150.5 5.0 %fusion.358 = (f32[2,4,128]{2,1,0:T(4,128)S(1)}, f32[2,4,128]{2,1,0:T(4,128)S(1)}, f32[2,4,128]{2,1,0:T(4,128)S(1)}, f32[2,4,128]{2,1,0:T(4,128)S(1)}, f32[2,4,1...) fusion(f32[2,4,128]{2,1,0:T(4,128)S(1)} %get-tuple-element.1734, ...), kind=kLoop, calls=%fused_computation.624 | loop fusion | flops 20029440 | bytes 180240 | tf_op jit(solution)/shard_map/transpose(jvp())/reduce_sum | solution.py:50
  155.8 1.8 collective-permute-start.8
  158.9 2.0 collective-permute-done.9
  161.2 1.9 collective-permute-start.11
  164.6 2.1 collective-permute-done.11
  167.3 2.0 fusion.396
  169.3 2.0 fusion.372
  171.3 2.0 fusion.384
  173.3 2.8 %fusion.360 = (f32[2,4,128]{2,1,0:T(4,128)S(1)}, f32[2,4,128]{2,1,0:T(4,128)S(1)}, f32[2,4,128]{2,1,0:T(4,128)S(1)}, f32[2,4,128]{2,1,0:T(4,128)S(1)}, f32[2,4,1...) fusion(f32[2,4,128]{2,1,0:T(4,128)S(1)} %get-tuple-element.1734, ...), kind=kLoop, calls=%fused_computation.626 | loop fusion | flops 11778048 | bytes 155664 | tf_op jit(solution)/shard_map/transpose(jvp())/reduce_sum | solution.py:50
  178.4 1.8 collective-permute-done.13
  180.6 28.3 %while.64 = (s32[]{:T(128)}, f32[3,1024]{1,0:T(4,128)S(1)}, f32[1024]{0:T(1024)S(1)}, f32[2,3,1024]{2,1,0:T(4,128)S(1)}, f32[2,3,1024]{2,1,0:T(4,128)S(1)}, /*in...) while((s32[]{:T(128)}, f32[3,1024]{1,0:T(4,128)S(1)}, ...), condition=%wide.region_74.75_spmd.clone, body=%wide.region_67.74_spmd.clone.sunk | while | flops 78705664 | bytes 426451 | solution.py:115
  181.1 13.6 %fusion.524 = (f32[1024]{0:T(1024)S(1)}, f32[1024]{0:T(1024)S(1)}, f32[1024]{0:T(1024)S(1)}, f32[1024]{0:T(1024)S(1)}, f32[1024]{0:T(1024)S(1)}, /*index=5*/f32[1024]{0:T(1024)S(1)}) fusion(f32[1024]{0:T(1024)S(1)} %bitcast.610, f32[1024]{0:T(1024)S(1)} %bitcast.619, f32[1024]{0:T(1024)S(1)} %bitcast.612, f32[1024]{0:T(1024)S(1)} %bitcast.621, ...), kind=kLoop, calls=%fused_computation.178.clone.1 | loop fusion | flops 78637056 | bytes 106496 | tf_op jit(solution)/shard_map/transpose(jvp())/while/body/eval_jaxpr/checkpoint/reduce_sum | solution.py:77
  195.2 13.6 %fusion.524 = (f32[1024]{0:T(1024)S(1)}, f32[1024]{0:T(1024)S(1)}, f32[1024]{0:T(1024)S(1)}, f32[1024]{0:T(1024)S(1)}, f32[1024]{0:T(1024)S(1)}, /*index=5*/f32[1024]{0:T(1024)S(1)}) fusion(f32[1024]{0:T(1024)S(1)} %bitcast.610, f32[1024]{0:T(1024)S(1)} %bitcast.619, f32[1024]{0:T(1024)S(1)} %bitcast.612, f32[1024]{0:T(1024)S(1)} %bitcast.621, ...), kind=kLoop, calls=%fused_computation.178.clone.1 | loop fusion | flops 78637056 | bytes 106496 | tf_op jit(solution)/shard_map/transpose(jvp())/while/body/eval_jaxpr/checkpoint/reduce_sum | solution.py:77
  210.4 2.0 collective-permute-start.15
  212.4 24.8 %reduce-scatter.7.cloned.1.call-done = f32[512,3]{1,0:T(8,128)} async-done(((f32[2048,3]{1,0:T(8,128)}), f32[512,3]{1,0:T(8,128)}) %reduce-scatter.7.cloned.1.call-update) | async-done | bytes 6160
  237.2 21.3 %reduce-scatter.9.cloned.1.call-done = f32[128,3]{1,0:T(8,128)} async-done(((f32[512,3]{1,0:T(8,128)}), f32[128,3]{1,0:T(8,128)}) %reduce-scatter.9.cloned.1.call-update) | async-done | bytes 1552
  (360 shorter events, 33.5 us)
Async XLA Ops:
  7.2 37.0 %copy-start = (f32[3,2,4,128]{3,2,1,0:T(4,128)S(1)}, f32[3,2,4,128]{3,2,1,0:T(4,128)}, u32[]{:S(2)}) copy-start(f32[3,2,4,128]{3,2,1,0:T(4,128)} %param.27) | copy-start | bytes 36868
  7.2 37.6 %copy-start.2 = (f32[2,4,128]{2,1,0:T(4,128)S(1)}, f32[2,4,128]{2,1,0:T(4,128)}, u32[]{:S(2)}) copy-start(f32[2,4,128]{2,1,0:T(4,128)} %param.29) | copy-start | bytes 12292
  7.2 37.6 %copy-start.3 = (f32[2,4,128]{2,1,0:T(4,128)S(1)}, f32[2,4,128]{2,1,0:T(4,128)}, u32[]{:S(2)}) copy-start(f32[2,4,128]{2,1,0:T(4,128)} %param.28) | copy-start | bytes 12292
  7.2 230.0 %reduce-scatter.7.cloned.1.call-start = ((), (), s32[]{:S(2)}) async-start(), calls=%async_computation.2 | async-start | bytes 1310720
  8.0 32.8 %collective-permute-start = (f32[5,1,4,128]{3,2,1,0:T(4,128)S(1)}, f32[5,1,4,128]{3,2,1,0:T(4,128)S(1)}, u32[]{:S(2)}, u32[]{:S(2)}) collective-permute-start(f32[5,1,4,128]{3,2,1,0:T(4,128)S(1)} %get-tuple-element.1764), channel_id=1, source_target_pairs={{0,4},{4,8},{8,12},{12,0},{1,5},{5,9},{9,13},{13,1},{2,6},{6,10},{... | collective-permute-start | bytes 30728 | tf_op jit(solution)/shard_map/ppermute | solution.py:26
  11.1 29.7 %collective-permute-start.1 = (f32[5,1,4,128]{3,2,1,0:T(4,128)S(1)}, f32[5,1,4,128]{3,2,1,0:T(4,128)S(1)}, u32[]{:S(2)}, u32[]{:S(2)}) collective-permute-start(f32[5,1,4,128]{3,2,1,0:T(4,128)S(1)} %get-tuple-element.1765), channel_id=1, source_target_pairs={{4,0},{8,4},{12,8},{0,12},{5,1},{9,5},{13,9},{1,13},{6,2},{10,6},{... | collective-permute-start | bytes 30728 | tf_op jit(solution)/shard_map/ppermute | solution.py:28
  41.6 3.1 %collective-permute-start.2 = (f32[5,4,1,128]{3,2,1,0:T(1,128)S(1)}, f32[5,4,1,128]{3,2,1,0:T(1,128)S(1)}, u32[]{:S(2)}, u32[]{:S(2)}) collective-permute-start(f32[5,4,1,128]{3,2,1,0:T(1,128)S(1)} %get-tuple-element.1746), channel_id=1, source_target_pairs={{0,1},{1,2},{2,3},{3,0},{4,5},{5,6},{6,7},{7,4},{8,9},{9,10},{10,1... | collective-permute-start | bytes 30728 | tf_op jit(solution)/shard_map/ppermute | solution.py:26
  41.7 24.1 %collective-permute-start.3 = (f32[5,4,1,128]{3,2,1,0:T(1,128)S(1)}, f32[5,4,1,128]{3,2,1,0:T(1,128)S(1)}, u32[]{:S(2)}, u32[]{:S(2)}) collective-permute-start(f32[5,4,1,128]{3,2,1,0:T(1,128)S(1)} %get-tuple-element.1747), channel_id=1, source_target_pairs={{1,0},{2,1},{3,2},{0,3},{5,4},{6,5},{7,6},{4,7},{9,8},{10,9},{11,1... | collective-permute-start | bytes 30728 | tf_op jit(solution)/shard_map/ppermute | solution.py:28
  44.9 28.9 %copy-start.1 = (s32[2,4,8]{2,1,0:T(4,128)S(1)}, s32[2,4,8]{2,1,0:T(4,128)}, u32[]{:S(2)}) copy-start(s32[2,4,8]{2,1,0:T(4,128)} %param.31) | copy-start | bytes 772
  69.9 65.8 %collective-permute-start.4 = (f32[1,4,128]{2,1,0:T(4,128)S(1)}, f32[1,4,128]{2,1,0:T(4,128)S(1)}, u32[]{:S(2)}, u32[]{:S(2)}) collective-permute-start(f32[1,4,128]{2,1,0:T(4,128)S(1)} %get-tuple-element.1813), channel_id=1, source_target_pairs={{0,4},{4,8},{8,12},{12,0},{1,5},{5,9},{9,13},{13,1},{2,6},{6,10},{... | collective-permute-start | bytes 6152 | tf_op jit(solution)/shard_map/ppermute | solution.py:26
  70.1 65.6 %collective-permute-start.5 = (f32[1,4,128]{2,1,0:T(4,128)S(1)}, f32[1,4,128]{2,1,0:T(4,128)S(1)}, u32[]{:S(2)}, u32[]{:S(2)}) collective-permute-start(f32[1,4,128]{2,1,0:T(4,128)S(1)} %get-tuple-element.1814), channel_id=1, source_target_pairs={{4,0},{8,4},{12,8},{0,12},{5,1},{9,5},{13,9},{1,13},{6,2},{10,6},{... | collective-permute-start | bytes 6152 | tf_op jit(solution)/shard_map/ppermute | solution.py:28
  135.6 31.0 %copy-start.4 = (f32[1024]{0:T(1024)}, f32[1024]{0:T(1024)S(1)}, u32[]{:S(2)}) copy-start(f32[1024]{0:T(1024)S(1)} %get-tuple-element.2483) | copy-start | bytes 12292
  135.7 3.1 %collective-permute-start.7 = (f32[4,1,128]{2,1,0:T(1,128)S(1)}, f32[4,1,128]{2,1,0:T(1,128)S(1)}, u32[]{:S(2)}, u32[]{:S(2)}) collective-permute-start(f32[4,1,128]{2,1,0:T(1,128)S(1)} %get-tuple-element.1809), channel_id=1, source_target_pairs={{0,1},{1,2},{2,3},{3,0},{4,5},{5,6},{6,7},{7,4},{8,9},{9,10},{10,1... | collective-permute-start | bytes 6152 | tf_op jit(solution)/shard_map/ppermute | solution.py:26
  135.8 3.0 %collective-permute-start.6 = (f32[4,1,128]{2,1,0:T(1,128)S(1)}, f32[4,1,128]{2,1,0:T(1,128)S(1)}, u32[]{:S(2)}, u32[]{:S(2)}) collective-permute-start(f32[4,1,128]{2,1,0:T(1,128)S(1)} %get-tuple-element.1810), channel_id=1, source_target_pairs={{1,0},{2,1},{3,2},{0,3},{5,4},{6,5},{7,6},{4,7},{9,8},{10,9},{11,1... | collective-permute-start | bytes 6152 | tf_op jit(solution)/shard_map/ppermute | solution.py:28
  155.8 3.1 %collective-permute-start.8 = (f32[1,4,128]{2,1,0:T(4,128)S(1)}, f32[1,4,128]{2,1,0:T(4,128)S(1)}, u32[]{:S(2)}, u32[]{:S(2)}) collective-permute-start(f32[1,4,128]{2,1,0:T(4,128)S(1)} %get-tuple-element.1794), channel_id=1, source_target_pairs={{0,3},{1,0},{2,1},{3,2},{4,7},{5,4},{6,5},{7,6},{8,11},{9,8},{10,9... | collective-permute-start | bytes 6152 | tf_op jit(solution)/shard_map/ppermute | solution.py:16
  157.8 3.1 %collective-permute-start.9 = (f32[1,4,128]{2,1,0:T(4,128)S(1)}, f32[1,4,128]{2,1,0:T(4,128)S(1)}, u32[]{:S(2)}, u32[]{:S(2)}) collective-permute-start(f32[1,4,128]{2,1,0:T(4,128)S(1)} %get-tuple-element.1793), channel_id=1, source_target_pairs={{0,1},{1,2},{2,3},{3,0},{4,5},{5,6},{6,7},{7,4},{8,9},{9,10},{10,1... | collective-permute-start | bytes 6152 | tf_op jit(solution)/shard_map/ppermute | solution.py:16
  160.9 3.6 %collective-permute-start.10 = (f32[1,4,128]{2,1,0:T(4,128)S(1)}, f32[1,4,128]{2,1,0:T(4,128)S(1)}, u32[]{:S(2)}, u32[]{:S(2)}) collective-permute-start(f32[1,4,128]{2,1,0:T(4,128)S(1)} %get-tuple-element.1808), channel_id=1, source_target_pairs={{0,12},{4,0},{8,4},{12,8},{1,13},{5,1},{9,5},{13,9},{2,14},{6,2},{... | collective-permute-start | bytes 6152 | tf_op jit(solution)/shard_map/ppermute | solution.py:16
  161.2 5.4 %collective-permute-start.11 = (f32[1,4,128]{2,1,0:T(4,128)S(1)}, f32[1,4,128]{2,1,0:T(4,128)S(1)}, u32[]{:S(2)}, u32[]{:S(2)}) collective-permute-start(f32[1,4,128]{2,1,0:T(4,128)S(1)} %get-tuple-element.1807), channel_id=1, source_target_pairs={{0,4},{4,8},{8,12},{12,0},{1,5},{5,9},{9,13},{13,1},{2,6},{6,10},{... | collective-permute-start | bytes 6152 | tf_op jit(solution)/shard_map/ppermute | solution.py:16
  177.0 1.4 collective-permute-start.12
  177.1 3.2 %collective-permute-start.13 = (f32[3,4,128]{2,0,1:T(4,128)S(1)}, f32[3,4,128]{2,0,1:T(4,128)S(1)}, u32[]{:S(2)}, u32[]{:S(2)}) collective-permute-start(f32[3,4,128]{2,0,1:T(4,128)S(1)} %get-tuple-element.1744), channel_id=1, source_target_pairs={{0,1},{1,2},{2,3},{3,0},{4,5},{5,6},{6,7},{7,4},{8,9},{9,10},{10,1... | collective-permute-start | bytes 18440 | tf_op jit(solution)/shard_map/ppermute | solution.py:16
  180.2 32.2 %collective-permute-start.14 = (f32[3,4,128]{2,0,1:T(4,128)S(1)}, f32[3,4,128]{2,0,1:T(4,128)S(1)}, u32[]{:S(2)}, u32[]{:S(2)}) collective-permute-start(f32[3,4,128]{2,0,1:T(4,128)S(1)} %get-tuple-element.1749), channel_id=1, source_target_pairs={{0,12},{4,0},{8,4},{12,8},{1,13},{5,1},{9,5},{13,9},{2,14},{6,2},{... | collective-permute-start | bytes 18440 | tf_op jit(solution)/shard_map/ppermute | solution.py:16
  210.3 49.2 %copy-start.5 = (s32[2,4,128]{2,1,0:T(4,128)S(1)}, s32[2,4,128]{2,1,0:T(4,128)}, u32[]{:S(2)}) copy-start(s32[2,4,128]{2,1,0:T(4,128)} %param.30) | copy-start | bytes 12292
  210.3 48.2 %reduce-scatter.9.cloned.1.call-start = ((), (), s32[]{:S(2)}) async-start(), calls=%async_computation.3 | async-start | bytes 327680
  210.4 26.8 %collective-permute-start.15 = (f32[3,4,128]{2,0,1:T(4,128)S(1)}, f32[3,4,128]{2,0,1:T(4,128)S(1)}, u32[]{:S(2)}, u32[]{:S(2)}) collective-permute-start(f32[3,4,128]{2,0,1:T(4,128)S(1)} %get-tuple-element.1748), channel_id=1, source_target_pairs={{0,4},{4,8},{8,12},{12,0},{1,5},{5,9},{9,13},{13,1},{2,6},{6,10},{... | collective-permute-start | bytes 18440 | tf_op jit(solution)/shard_map/ppermute | solution.py:16
Sparse Core Ops, SparseCore 0:
  210.4 26.7 reduce-scatter.6
  239.8 18.7 reduce-scatter.8
where the time goes:
time: 268 us; the launch traced here: 267 us
  other arithmetic  146 us (54%)
  waiting for transfers between devices  57.1 us (21%)
  starting transfers between devices  19.6 us (7%)
  blocking collectives  18.3 us (7%)
  between operations  15.6 us (6%)
  local copies, waits for them, and re-layouts  6.67 us (2%)
  matrix products  3.78 us (1%)
    reduce_sum x4, other arithmetic, centre_distance(): apart_axis = flat_pos[axis_slot][:, None] - centre[axis_slot][None, :]  59 us
    unnamed x4, waiting for transfers between devices  46.1 us
    reduce_sum x2, other arithmetic, potential_block(): product = flat_born[:, None] * comp_radius[None, :]  28.8 us
    reduce_sum x8, other arithmetic, pair_distance(): own_pos[axis_slot][..., :, None] - part_pos[axis_slot][..., None, :]  25.1 us
    reduce_sum x2, other arithmetic, screen_block(): jnp.sum(jnp.where(keep, volume * weight / (denom_sq * denom_sq), 0.0), ax...  19.9 us
    all_gather x1, blocking collectives, local(): all_table = lax.all_gather(sub_table, 'dom', axis=1, tiled=True)  13.1 us
    ppermute x4, starting transfers between devices, extended(): lax.ppermute(head, axis, [((i + 1) % count, i) for i in range(count)])  9.21 us
    ppermute x8, waiting for transfers between devices, passed_along(): lax.ppermute(shard, axis, [(i, (i + by) % size) for i in range(size)])  9.12 us
  transfers between devices with their start and end apart: 18, of which 10 were waited for; matrix products, arithmetic and copies ran while one was open for 46% of the time, Pallas kernels for 0%

commit v1 on v0

--- a/solution.py
+++ b/solution.py
@@ -201,7 +201,24 @@
         axis=0,
     )
     sub_table = lax.all_gather(comp_table, "sub", axis=1, tiled=True)
-    all_table = lax.all_gather(sub_table, "dom", axis=1, tiled=True)
+    size_2, index, rows = (lax.axis_size("dom"), lax.axis_index("dom"), sub_table.shape[1])
+    forward = [(i_2, (i_2 + 1) % size_2) for i_2 in range(size_2)]
+    left = [(i_2, (i_2 - 1) % size_2) for i_2 in range(size_2)]
+    out = jnp.zeros(
+        (*sub_table.shape[:1], size_2 * rows, *sub_table.shape[1 + 1 :]), sub_table.dtype
+    )
+    out = lax.dynamic_update_slice_in_dim(out, sub_table, index * rows, axis=1)
+    from_left = from_right = sub_table
+    half = size_2 // 2
+    for lap in range(1, half + 1):
+        from_left = lax.ppermute(from_left, "dom", forward)
+        out = lax.dynamic_update_slice_in_dim(out, from_left, (index - lap) % size_2 * rows, axis=1)
+        if lap < size_2 - half:
+            from_right = lax.ppermute(from_right, "dom", left)
+            out = lax.dynamic_update_slice_in_dim(
+                out, from_right, (index + lap) % size_2 * rows, axis=1
+            )
+    all_table = out
     all_centre = all_table[0:3]
     all_charge = all_table[3]
     all_volume = all_table[4]

time: 268 us -> 266 us (level)
  blocking collectives: 18.3 us -> 6.19 us
  starting transfers between devices: 19.6 us -> 24.7 us
  waiting for transfers between devices: 57.1 us -> 61.2 us
    all_gather x1 -> x0, blocking collectives: 13.1 us -> none  [local(): all_table = lax.all_gather(sub_table, 'dom', axis=1, tiled=True)]
    ppermute x0 -> x3, starting transfers between devices: none -> 4.11 us  [the longest x1 4.05 us: local(): from_right = lax.ppermute(from_right, 'dom', left)]
    ppermute x4, starting transfers between devices: 3.4 us -> 0.41 us  [extended(): lax.ppermute(tail, axis, [(i, (i + 1) % count) for i in range(count)])]
  transfers between devices with their start and end apart: 18 -> 21, of which waited for: 10 -> 11; matrix products, arithmetic and copies ran while one was open for 46% -> 39% of each run, Pallas kernels for 0% -> 0%
where the time goes in v1:
time: 266 us; the launch traced here: 265 us
  other arithmetic  146 us (55%)
  waiting for transfers between devices  61.2 us (23%)
  starting transfers between devices  24.7 us (9%)
  between operations  15.8 us (6%)
  local copies, waits for them, and re-layouts  6.7 us (3%)
  blocking collectives  6.19 us (2%)
  matrix products  3.78 us (1%)
    reduce_sum x4, other arithmetic, centre_distance(): apart_axis = flat_pos[axis_slot][:, None] - centre[axis_slot][None, :]  59 us
    unnamed x4, waiting for transfers between devices  46.1 us
    reduce_sum x2, other arithmetic, potential_block(): product = flat_born[:, None] * comp_radius[None, :]  28.8 us
    reduce_sum x8, other arithmetic, pair_distance(): own_pos[axis_slot][..., :, None] - part_pos[axis_slot][..., None, :]  25 us
    reduce_sum x2, other arithmetic, screen_block(): jnp.sum(jnp.where(keep, volume * weight / (denom_sq * denom_sq), 0.0), ax...  20 us
    ppermute x4, starting transfers between devices, extended(): lax.ppermute(head, axis, [((i + 1) % count, i) for i in range(count)])  11.4 us
    ppermute x8, waiting for transfers between devices, passed_along(): lax.ppermute(shard, axis, [(i, (i + by) % size) for i in range(size)])  11 us
    ppermute x8, starting transfers between devices, passed_along(): lax.ppermute(shard, axis, [(i, (i + by) % size) for i in range(size)])  8.68 us
  transfers between devices with their start and end apart: 21, of which 11 were waited for; matrix products, arithmetic and copies ran while one was open for 39% of the time, Pallas kernels for 0%

profile of v1, /device:TPU:0, one launch (start us, length us, event | category | flops | bytes accessed | tf_op | source)
XLA Modules:
  0.0 265.3 jit_solution(5730360558600535846)
XLA Ops:
  12.6 6.2 %all_gather.3 = f32[6,512]{1,0:T(8,128)S(1)} all-gather(f32[6,128]{1,0:T(8,128)S(1)} %pad_maximum_fusion.40), channel_id=1, replica_groups=mesh['groups'=2,'dom'=4,'sub'=4] {'sub'}, dimensions={1}, use_global_device_ids=true | all-gather | bytes 15360 | tf_op jit(solution)/shard_map/all_gather | solution.py:203
  18.8 4.0 %collective-permute-start.5 = (f32[6,512]{1,0:T(8,128)S(1)}, f32[6,512]{1,0:T(8,128)S(1)}, u32[]{:S(2)}, u32[]{:S(2)}) collective-permute-start(f32[6,512]{1,0:T(8,128)S(1)} %all_gather.3), channel_id=1, source_target_pairs={{0,12},{4,0},{8,4},{12,8},{1,13},{5,1},{9,5},{13,9},{2,14},{6,2},{... | collective-permute-start | bytes 36872 | tf_op jit(solution)/shard_map/ppermute | solution.py:217
  23.7 3.9 %collective-permute-start.1 = (f32[5,1,4,128]{3,2,1,0:T(4,128)S(1)}, f32[5,1,4,128]{3,2,1,0:T(4,128)S(1)}, u32[]{:S(2)}, u32[]{:S(2)}) collective-permute-start(f32[5,1,4,128]{3,2,1,0:T(4,128)S(1)} %get-tuple-element.1765), channel_id=1, source_target_pairs={{4,0},{8,4},{12,8},{0,12},{5,1},{9,5},{13,9},{1,13},{6,2},{10,6},{... | collective-permute-start | bytes 30728 | tf_op jit(solution)/shard_map/ppermute | solution.py:28
  41.3 21.0 %while.65 = (s32[]{:T(128)}, f32[1024]{0:T(1024)S(1)}, s32[2,1024]{1,0:T(2,128)S(1)}, s32[2,1024]{1,0:T(2,128)S(1)}, pred[1024,1]{0,1:T(4,128)(4,1)S(1)}, /*inde...) while((s32[]{:T(128)}, f32[1024]{0:T(1024)S(1)}, ...), condition=%wide.region_12.13_spmd.clone.clone.clone, body=%wide.region_10.12_spmd.clone.clone.clone.sunk | while | flops 50371588 | bytes 205115 | solution.py:115
  41.8 10.0 %select_reduce_fusion.11 = f32[1024]{0:T(1024)S(1)} fusion(f32[1024]{0:T(1024)S(1)} %bitcast.621, f32[1024]{0:T(1024)S(1)} %bitcast.591, f32[1024]{0:T(1024)S(1)} %bitcast.694, f32[1024]{0:T(1024)S(1)} %bitcast.590, f32[1024]{0:T(1024)S(1)} %bitcast.692, f32[1024]{0:T(1024)S(1)} %bitcast.589, f32[1024]{0:T(1024)S(1)} %bitcast.690, ...), kind=kLoop, calls=%fused_computation.229.clone.1 | loop fusion | flops 50330624 | bytes 81920 | tf_op jit(solution)/shard_map/jvp()/while/body/eval_jaxpr/reduce_sum | solution.py:86
  52.3 10.0 %select_reduce_fusion.11 = f32[1024]{0:T(1024)S(1)} fusion(f32[1024]{0:T(1024)S(1)} %bitcast.621, f32[1024]{0:T(1024)S(1)} %bitcast.591, f32[1024]{0:T(1024)S(1)} %bitcast.694, f32[1024]{0:T(1024)S(1)} %bitcast.590, f32[1024]{0:T(1024)S(1)} %bitcast.692, f32[1024]{0:T(1024)S(1)} %bitcast.589, f32[1024]{0:T(1024)S(1)} %bitcast.690, ...), kind=kLoop, calls=%fused_computation.229.clone.1 | loop fusion | flops 50330624 | bytes 81920 | tf_op jit(solution)/shard_map/jvp()/while/body/eval_jaxpr/reduce_sum | solution.py:86
  62.4 3.8 %collective-permute-start.8 = (f32[1,4,128]{2,1,0:T(4,128)S(1)}, f32[1,4,128]{2,1,0:T(4,128)S(1)}, u32[]{:S(2)}, u32[]{:S(2)}) collective-permute-start(f32[1,4,128]{2,1,0:T(4,128)S(1)} %get-tuple-element.1814), channel_id=1, source_target_pairs={{4,0},{8,4},{12,8},{0,12},{5,1},{9,5},{13,9},{1,13},{6,2},{10,6},{... | collective-permute-start | bytes 6152 | tf_op jit(solution)/shard_map/ppermute | solution.py:28
  68.1 61.9 %while.63 = (s32[]{:T(128)}, f32[3,1024]{1,0:T(4,128)S(1)}, f32[1024]{0:T(1024)S(1)}, f32[1024]{0:T(1024)S(1)}, f32[2,3,1024]{2,1,0:T(4,128)S(1)}, /*index=5*/f3...) while((s32[]{:T(128)}, f32[3,1024]{1,0:T(4,128)S(1)}, ...), condition=%wide.region_21.22_spmd.clone, body=%wide.region_13.21_spmd.clone.sunk | while | flops 160494592 | bytes 520676 | solution.py:139
  68.6 14.4 %multiply_reduce_fusion.20 = f32[1024]{0:T(1024)S(1)} fusion(f32[1024]{0:T(1024)S(1)} %bitcast.598, f32[1024]{0:T(1024)S(1)} %get-tuple-element.2180, f32[1024]{0:T(1024)S(1)} %bitcast.605, f32[1024]{0:T(1024)S(1)} %bitcast.614, f32[1024]{0:T(1024)S(1)} %bitcast.607, f32[1024]{0:T(1024)S(1)} %bitcast.616, f32[1024]{0:T(1024)S(1)} %bitcast.603, ...), kind=kLoop, calls=%fused_computation.76.clone.1 | loop fusion | flops 72350720 | bytes 90112 | tf_op jit(solution)/shard_map/transpose(jvp())/while/body/eval_jaxpr/checkpoint/reduce_sum | solution.py:92
  82.9 16.0 %fusion.518 = (f32[1024]{0:T(1024)S(1)}, f32[1024]{0:T(1024)S(1)}, f32[1024]{0:T(1024)S(1)}, f32[1024]{0:T(1024)S(1)}, f32[1024]{0:T(1024)S(1)}, /*index=5*/f32[1024]{0:T(1024)S(1)}) fusion(f32[1024]{0:T(1024)S(1)} %bitcast.604, f32[1024]{0:T(1024)S(1)} %bitcast.613, f32[1024]{0:T(1024)S(1)} %bitcast.608, f32[1024]{0:T(1024)S(1)} %bitcast.617, ...), kind=kLoop, calls=%fused_computation.89.clone.1 | loop fusion | flops 88074240 | bytes 110592 | tf_op jit(solution)/shard_map/transpose(jvp())/while/body/eval_jaxpr/checkpoint/reduce_sum | solution.py:77
  99.5 14.4 %multiply_reduce_fusion.20 = f32[1024]{0:T(1024)S(1)} fusion(f32[1024]{0:T(1024)S(1)} %bitcast.598, f32[1024]{0:T(1024)S(1)} %get-tuple-element.2180, f32[1024]{0:T(1024)S(1)} %bitcast.605, f32[1024]{0:T(1024)S(1)} %bitcast.614, f32[1024]{0:T(1024)S(1)} %bitcast.607, f32[1024]{0:T(1024)S(1)} %bitcast.616, f32[1024]{0:T(1024)S(1)} %bitcast.603, ...), kind=kLoop, calls=%fused_computation.76.clone.1 | loop fusion | flops 72350720 | bytes 90112 | tf_op jit(solution)/shard_map/transpose(jvp())/while/body/eval_jaxpr/checkpoint/reduce_sum | solution.py:92
  113.9 16.0 %fusion.518 = (f32[1024]{0:T(1024)S(1)}, f32[1024]{0:T(1024)S(1)}, f32[1024]{0:T(1024)S(1)}, f32[1024]{0:T(1024)S(1)}, f32[1024]{0:T(1024)S(1)}, /*index=5*/f32[1024]{0:T(1024)S(1)}) fusion(f32[1024]{0:T(1024)S(1)} %bitcast.604, f32[1024]{0:T(1024)S(1)} %bitcast.613, f32[1024]{0:T(1024)S(1)} %bitcast.608, f32[1024]{0:T(1024)S(1)} %bitcast.617, ...), kind=kLoop, calls=%fused_computation.89.clone.1 | loop fusion | flops 88074240 | bytes 110592 | tf_op jit(solution)/shard_map/transpose(jvp())/while/body/eval_jaxpr/checkpoint/reduce_sum | solution.py:77
  130.0 2.0 collective-permute-start.9
  133.3 3.7 %fusion.382 = (f32[2,4,128]{2,1,0:T(4,128)S(1)}, f32[2,4,128]{2,1,0:T(4,128)S(1)}, f32[2,4,128]{2,1,0:T(4,128)S(1)}, f32[2,4,128]{2,1,0:T(4,128)S(1)}, f32[2,4,1...) fusion(f32[2,4,128]{2,1,0:T(4,128)S(1)} %get-tuple-element.1743, ...), kind=kLoop, calls=%fused_computation.648 | loop fusion | flops 13352960 | bytes 126992 | tf_op jit(solution)/shard_map/transpose(jvp())/reduce_sum | solution.py:50
  137.2 3.7 %fusion.406 = (f32[2,4,128]{2,1,0:T(4,128)S(1)}, f32[2,4,128]{2,1,0:T(4,128)S(1)}, f32[2,4,128]{2,1,0:T(4,128)S(1)}, f32[2,4,128]{2,1,0:T(4,128)S(1)}, f32[2,4,1...) fusion(f32[2,4,128]{2,1,0:T(4,128)S(1)} %get-tuple-element.1739, ...), kind=kLoop, calls=%fused_computation.672 | loop fusion | flops 13352960 | bytes 126992 | tf_op jit(solution)/shard_map/transpose(jvp())/reduce_sum | solution.py:50
  141.1 3.7 %fusion.430 = (f32[2,4,128]{2,1,0:T(4,128)S(1)}, f32[2,4,128]{2,1,0:T(4,128)S(1)}, f32[2,4,128]{2,1,0:T(4,128)S(1)}, f32[2,4,128]{2,1,0:T(4,128)S(1)}, f32[2,4,1...) fusion(f32[2,4,128]{2,1,0:T(4,128)S(1)} %get-tuple-element.1759, ...), kind=kLoop, calls=%fused_computation.696 | loop fusion | flops 13352960 | bytes 126992 | tf_op jit(solution)/shard_map/transpose(jvp())/reduce_sum | solution.py:50
  145.0 5.0 %fusion.358 = (f32[2,4,128]{2,1,0:T(4,128)S(1)}, f32[2,4,128]{2,1,0:T(4,128)S(1)}, f32[2,4,128]{2,1,0:T(4,128)S(1)}, f32[2,4,128]{2,1,0:T(4,128)S(1)}, f32[2,4,1...) fusion(f32[2,4,128]{2,1,0:T(4,128)S(1)} %get-tuple-element.1734, ...), kind=kLoop, calls=%fused_computation.624 | loop fusion | flops 20029440 | bytes 180240 | tf_op jit(solution)/shard_map/transpose(jvp())/reduce_sum | solution.py:50
  150.3 1.8 collective-permute-start.11
  153.3 2.0 collective-permute-done.12
  155.4 3.9 %collective-permute-start.13 = (f32[1,4,128]{2,1,0:T(4,128)S(1)}, f32[1,4,128]{2,1,0:T(4,128)S(1)}, u32[]{:S(2)}, u32[]{:S(2)}) collective-permute-start(f32[1,4,128]{2,1,0:T(4,128)S(1)} %get-tuple-element.1808), channel_id=1, source_target_pairs={{0,12},{4,0},{8,4},{12,8},{1,13},{5,1},{9,5},{13,9},{2,14},{6,2},{... | collective-permute-start | bytes 6152 | tf_op jit(solution)/shard_map/ppermute | solution.py:16
  160.6 4.1 %collective-permute-done.14 = f32[1,4,128]{2,1,0:T(4,128)S(1)} collective-permute-done((f32[1,4,128]{2,1,0:T(4,128)S(1)}, f32[1,4,128]{2,1,0:T(4,128)S(1)}, u32[]{:S(2)}, u32[]{:S(2)}) %collective-permute-start.14) | collective-permute-done | bytes 2080 | tf_op jit(solution)/shard_map/ppermute | solution.py:16
  165.3 2.0 fusion.396
  167.3 2.0 fusion.372
  169.4 2.0 fusion.384
  171.4 2.8 %fusion.360 = (f32[2,4,128]{2,1,0:T(4,128)S(1)}, f32[2,4,128]{2,1,0:T(4,128)S(1)}, f32[2,4,128]{2,1,0:T(4,128)S(1)}, f32[2,4,128]{2,1,0:T(4,128)S(1)}, f32[2,4,1...) fusion(f32[2,4,128]{2,1,0:T(4,128)S(1)} %get-tuple-element.1734, ...), kind=kLoop, calls=%fused_computation.626 | loop fusion | flops 11778048 | bytes 155664 | tf_op jit(solution)/shard_map/transpose(jvp())/reduce_sum | solution.py:50
  176.5 1.8 collective-permute-done.16
  178.6 28.3 %while.64 = (s32[]{:T(128)}, f32[3,1024]{1,0:T(4,128)S(1)}, f32[1024]{0:T(1024)S(1)}, f32[2,3,1024]{2,1,0:T(4,128)S(1)}, f32[2,3,1024]{2,1,0:T(4,128)S(1)}, /*in...) while((s32[]{:T(128)}, f32[3,1024]{1,0:T(4,128)S(1)}, ...), condition=%wide.region_74.75_spmd.clone, body=%wide.region_67.74_spmd.clone.sunk | while | flops 78705664 | bytes 426451 | solution.py:115
  179.1 13.6 %fusion.521 = (f32[1024]{0:T(1024)S(1)}, f32[1024]{0:T(1024)S(1)}, f32[1024]{0:T(1024)S(1)}, f32[1024]{0:T(1024)S(1)}, f32[1024]{0:T(1024)S(1)}, /*index=5*/f32[1024]{0:T(1024)S(1)}) fusion(f32[1024]{0:T(1024)S(1)} %bitcast.609, f32[1024]{0:T(1024)S(1)} %bitcast.618, f32[1024]{0:T(1024)S(1)} %bitcast.611, f32[1024]{0:T(1024)S(1)} %bitcast.620, ...), kind=kLoop, calls=%fused_computation.178.clone.1 | loop fusion | flops 78637056 | bytes 106496 | tf_op jit(solution)/shard_map/transpose(jvp())/while/body/eval_jaxpr/checkpoint/reduce_sum | solution.py:77
  193.3 13.6 %fusion.521 = (f32[1024]{0:T(1024)S(1)}, f32[1024]{0:T(1024)S(1)}, f32[1024]{0:T(1024)S(1)}, f32[1024]{0:T(1024)S(1)}, f32[1024]{0:T(1024)S(1)}, /*index=5*/f32[1024]{0:T(1024)S(1)}) fusion(f32[1024]{0:T(1024)S(1)} %bitcast.609, f32[1024]{0:T(1024)S(1)} %bitcast.618, f32[1024]{0:T(1024)S(1)} %bitcast.611, f32[1024]{0:T(1024)S(1)} %bitcast.620, ...), kind=kLoop, calls=%fused_computation.178.clone.1 | loop fusion | flops 78637056 | bytes 106496 | tf_op jit(solution)/shard_map/transpose(jvp())/while/body/eval_jaxpr/checkpoint/reduce_sum | solution.py:77
  208.4 2.0 collective-permute-start.18
  210.5 24.8 %reduce-scatter.7.cloned.1.call-done = f32[512,3]{1,0:T(8,128)} async-done(((f32[2048,3]{1,0:T(8,128)}), f32[512,3]{1,0:T(8,128)}) %reduce-scatter.7.cloned.1.call-update) | async-done | bytes 6160
  235.3 21.3 %reduce-scatter.9.cloned.1.call-done = f32[128,3]{1,0:T(8,128)} async-done(((f32[512,3]{1,0:T(8,128)}), f32[128,3]{1,0:T(8,128)}) %reduce-scatter.9.cloned.1.call-update) | async-done | bytes 1552
  (370 shorter events, 34.5 us)
Async XLA Ops:
  7.2 28.5 %copy-start.2 = (f32[2,4,128]{2,1,0:T(4,128)S(1)}, f32[2,4,128]{2,1,0:T(4,128)}, u32[]{:S(2)}) copy-start(f32[2,4,128]{2,1,0:T(4,128)} %param.29) | copy-start | bytes 12292
  7.2 28.5 %copy-start.3 = (f32[2,4,128]{2,1,0:T(4,128)S(1)}, f32[2,4,128]{2,1,0:T(4,128)}, u32[]{:S(2)}) copy-start(f32[2,4,128]{2,1,0:T(4,128)} %param.28) | copy-start | bytes 12292
  7.2 28.5 %copy-start = (f32[3,2,4,128]{3,2,1,0:T(4,128)S(1)}, f32[3,2,4,128]{3,2,1,0:T(4,128)}, u32[]{:S(2)}) copy-start(f32[3,2,4,128]{3,2,1,0:T(4,128)} %param.27) | copy-start | bytes 36868
  7.2 228.0 %reduce-scatter.7.cloned.1.call-start = ((), (), s32[]{:S(2)}) async-start(), calls=%async_computation.2 | async-start | bytes 1310720
  18.8 16.8 %collective-permute-start.5 = (f32[6,512]{1,0:T(8,128)S(1)}, f32[6,512]{1,0:T(8,128)S(1)}, u32[]{:S(2)}, u32[]{:S(2)}) collective-permute-start(f32[6,512]{1,0:T(8,128)S(1)} %all_gather.3), channel_id=1, source_target_pairs={{0,12},{4,0},{8,4},{12,8},{1,13},{5,1},{9,5},{13,9},{2,14},{6,2},{... | collective-permute-start | bytes 36872 | tf_op jit(solution)/shard_map/ppermute | solution.py:217
  22.9 12.7 %collective-permute-start.4 = (f32[6,512]{1,0:T(8,128)S(1)}, f32[6,512]{1,0:T(8,128)S(1)}, u32[]{:S(2)}, u32[]{:S(2)}) collective-permute-start(f32[6,512]{1,0:T(8,128)S(1)} %all_gather.3), channel_id=1, source_target_pairs={{0,4},{4,8},{8,12},{12,0},{1,5},{5,9},{9,13},{13,1},{2,6},{6,10},{... | collective-permute-start | bytes 36872 | tf_op jit(solution)/shard_map/ppermute | solution.py:214
  23.6 7.9 %collective-permute-start = (f32[5,1,4,128]{3,2,1,0:T(4,128)S(1)}, f32[5,1,4,128]{3,2,1,0:T(4,128)S(1)}, u32[]{:S(2)}, u32[]{:S(2)}) collective-permute-start(f32[5,1,4,128]{3,2,1,0:T(4,128)S(1)} %get-tuple-element.1764), channel_id=1, source_target_pairs={{0,4},{4,8},{8,12},{12,0},{1,5},{5,9},{9,13},{13,1},{2,6},{6,10},{... | collective-permute-start | bytes 30728 | tf_op jit(solution)/shard_map/ppermute | solution.py:26
  23.7 7.8 %collective-permute-start.1 = (f32[5,1,4,128]{3,2,1,0:T(4,128)S(1)}, f32[5,1,4,128]{3,2,1,0:T(4,128)S(1)}, u32[]{:S(2)}, u32[]{:S(2)}) collective-permute-start(f32[5,1,4,128]{3,2,1,0:T(4,128)S(1)} %get-tuple-element.1765), channel_id=1, source_target_pairs={{4,0},{8,4},{12,8},{0,12},{5,1},{9,5},{13,9},{1,13},{6,2},{10,6},{... | collective-permute-start | bytes 30728 | tf_op jit(solution)/shard_map/ppermute | solution.py:28
  32.3 3.4 %collective-permute-start.2 = (f32[5,4,1,128]{3,2,1,0:T(1,128)S(1)}, f32[5,4,1,128]{3,2,1,0:T(1,128)S(1)}, u32[]{:S(2)}, u32[]{:S(2)}) collective-permute-start(f32[5,4,1,128]{3,2,1,0:T(1,128)S(1)} %get-tuple-element.1746), channel_id=1, source_target_pairs={{0,1},{1,2},{2,3},{3,0},{4,5},{5,6},{6,7},{7,4},{8,9},{9,10},{10,1... | collective-permute-start | bytes 30728 | tf_op jit(solution)/shard_map/ppermute | solution.py:26
  32.4 3.3 %collective-permute-start.3 = (f32[5,4,1,128]{3,2,1,0:T(1,128)S(1)}, f32[5,4,1,128]{3,2,1,0:T(1,128)S(1)}, u32[]{:S(2)}, u32[]{:S(2)}) collective-permute-start(f32[5,4,1,128]{3,2,1,0:T(1,128)S(1)} %get-tuple-element.1747), channel_id=1, source_target_pairs={{1,0},{2,1},{3,2},{0,3},{5,4},{6,5},{7,6},{4,7},{9,8},{10,9},{11,1... | collective-permute-start | bytes 30728 | tf_op jit(solution)/shard_map/ppermute | solution.py:28
  35.6 5.6 %collective-permute-start.6 = (f32[6,512]{1,0:T(8,128)S(1)}, f32[6,512]{1,0:T(8,128)S(1)}, u32[]{:S(2)}, u32[]{:S(2)}) collective-permute-start(f32[6,512]{1,0:T(8,128)S(1)} %collective-permute-done.4), channel_id=1, source_target_pairs={{0,4},{4,8},{8,12},{12,0},{1,5},{5,9},{9,13},{13,1},{2,6},{6,10},{... | collective-permute-start | bytes 36872 | tf_op jit(solution)/shard_map/ppermute | solution.py:214
  41.3 26.8 %copy-start.1 = (s32[2,4,8]{2,1,0:T(4,128)S(1)}, s32[2,4,8]{2,1,0:T(4,128)}, u32[]{:S(2)}) copy-start(s32[2,4,8]{2,1,0:T(4,128)} %param.31) | copy-start | bytes 772
  62.4 5.4 %collective-permute-start.7 = (f32[1,4,128]{2,1,0:T(4,128)S(1)}, f32[1,4,128]{2,1,0:T(4,128)S(1)}, u32[]{:S(2)}, u32[]{:S(2)}) collective-permute-start(f32[1,4,128]{2,1,0:T(4,128)S(1)} %get-tuple-element.1813), channel_id=1, source_target_pairs={{0,4},{4,8},{8,12},{12,0},{1,5},{5,9},{9,13},{13,1},{2,6},{6,10},{... | collective-permute-start | bytes 6152 | tf_op jit(solution)/shard_map/ppermute | solution.py:26
  62.4 5.4 %collective-permute-start.8 = (f32[1,4,128]{2,1,0:T(4,128)S(1)}, f32[1,4,128]{2,1,0:T(4,128)S(1)}, u32[]{:S(2)}, u32[]{:S(2)}) collective-permute-start(f32[1,4,128]{2,1,0:T(4,128)S(1)} %get-tuple-element.1814), channel_id=1, source_target_pairs={{4,0},{8,4},{12,8},{0,12},{5,1},{9,5},{13,9},{1,13},{6,2},{10,6},{... | collective-permute-start | bytes 6152 | tf_op jit(solution)/shard_map/ppermute | solution.py:28
  67.8 64.1 %collective-permute-start.10 = (f32[4,1,128]{2,1,0:T(1,128)S(1)}, f32[4,1,128]{2,1,0:T(1,128)S(1)}, u32[]{:S(2)}, u32[]{:S(2)}) collective-permute-start(f32[4,1,128]{2,1,0:T(1,128)S(1)} %get-tuple-element.1809), channel_id=1, source_target_pairs={{0,1},{1,2},{2,3},{3,0},{4,5},{5,6},{6,7},{7,4},{8,9},{9,10},{10,1... | collective-permute-start | bytes 6152 | tf_op jit(solution)/shard_map/ppermute | solution.py:26
  129.9 34.8 %copy-start.4 = (f32[1024]{0:T(1024)}, f32[1024]{0:T(1024)S(1)}, u32[]{:S(2)}) copy-start(f32[1024]{0:T(1024)S(1)} %get-tuple-element.2483) | copy-start | bytes 12292
  130.0 3.3 %collective-permute-start.9 = (f32[4,1,128]{2,1,0:T(1,128)S(1)}, f32[4,1,128]{2,1,0:T(1,128)S(1)}, u32[]{:S(2)}, u32[]{:S(2)}) collective-permute-start(f32[4,1,128]{2,1,0:T(1,128)S(1)} %get-tuple-element.1810), channel_id=1, source_target_pairs={{1,0},{2,1},{3,2},{0,3},{5,4},{6,5},{7,6},{4,7},{9,8},{10,9},{11,1... | collective-permute-start | bytes 6152 | tf_op jit(solution)/shard_map/ppermute | solution.py:28
  150.3 3.1 %collective-permute-start.11 = (f32[1,4,128]{2,1,0:T(4,128)S(1)}, f32[1,4,128]{2,1,0:T(4,128)S(1)}, u32[]{:S(2)}, u32[]{:S(2)}) collective-permute-start(f32[1,4,128]{2,1,0:T(4,128)S(1)} %get-tuple-element.1794), channel_id=1, source_target_pairs={{0,3},{1,0},{2,1},{3,2},{4,7},{5,4},{6,5},{7,6},{8,11},{9,8},{10,9... | collective-permute-start | bytes 6152 | tf_op jit(solution)/shard_map/ppermute | solution.py:16
  152.3 3.1 %collective-permute-start.12 = (f32[1,4,128]{2,1,0:T(4,128)S(1)}, f32[1,4,128]{2,1,0:T(4,128)S(1)}, u32[]{:S(2)}, u32[]{:S(2)}) collective-permute-start(f32[1,4,128]{2,1,0:T(4,128)S(1)} %get-tuple-element.1793), channel_id=1, source_target_pairs={{0,1},{1,2},{2,3},{3,0},{4,5},{5,6},{6,7},{7,4},{8,9},{9,10},{10,1... | collective-permute-start | bytes 6152 | tf_op jit(solution)/shard_map/ppermute | solution.py:16
  155.4 5.2 %collective-permute-start.13 = (f32[1,4,128]{2,1,0:T(4,128)S(1)}, f32[1,4,128]{2,1,0:T(4,128)S(1)}, u32[]{:S(2)}, u32[]{:S(2)}) collective-permute-start(f32[1,4,128]{2,1,0:T(4,128)S(1)} %get-tuple-element.1808), channel_id=1, source_target_pairs={{0,12},{4,0},{8,4},{12,8},{1,13},{5,1},{9,5},{13,9},{2,14},{6,2},{... | collective-permute-start | bytes 6152 | tf_op jit(solution)/shard_map/ppermute | solution.py:16
  159.3 5.4 %collective-permute-start.14 = (f32[1,4,128]{2,1,0:T(4,128)S(1)}, f32[1,4,128]{2,1,0:T(4,128)S(1)}, u32[]{:S(2)}, u32[]{:S(2)}) collective-permute-start(f32[1,4,128]{2,1,0:T(4,128)S(1)} %get-tuple-element.1807), channel_id=1, source_target_pairs={{0,4},{4,8},{8,12},{12,0},{1,5},{5,9},{9,13},{13,1},{2,6},{6,10},{... | collective-permute-start | bytes 6152 | tf_op jit(solution)/shard_map/ppermute | solution.py:16
  175.0 1.4 collective-permute-start.15
  175.1 3.2 %collective-permute-start.16 = (f32[3,4,128]{2,0,1:T(4,128)S(1)}, f32[3,4,128]{2,0,1:T(4,128)S(1)}, u32[]{:S(2)}, u32[]{:S(2)}) collective-permute-start(f32[3,4,128]{2,0,1:T(4,128)S(1)} %get-tuple-element.1744), channel_id=1, source_target_pairs={{0,1},{1,2},{2,3},{3,0},{4,5},{5,6},{6,7},{7,4},{8,9},{9,10},{10,1... | collective-permute-start | bytes 18440 | tf_op jit(solution)/shard_map/ppermute | solution.py:16
  178.3 32.2 %collective-permute-start.17 = (f32[3,4,128]{2,0,1:T(4,128)S(1)}, f32[3,4,128]{2,0,1:T(4,128)S(1)}, u32[]{:S(2)}, u32[]{:S(2)}) collective-permute-start(f32[3,4,128]{2,0,1:T(4,128)S(1)} %get-tuple-element.1749), channel_id=1, source_target_pairs={{0,12},{4,0},{8,4},{12,8},{1,13},{5,1},{9,5},{13,9},{2,14},{6,2},{... | collective-permute-start | bytes 18440 | tf_op jit(solution)/shard_map/ppermute | solution.py:16
  208.3 49.2 %copy-start.5 = (s32[2,4,128]{2,1,0:T(4,128)S(1)}, s32[2,4,128]{2,1,0:T(4,128)}, u32[]{:S(2)}) copy-start(s32[2,4,128]{2,1,0:T(4,128)} %param.30) | copy-start | bytes 12292
  208.4 48.2 %reduce-scatter.9.cloned.1.call-start = ((), (), s32[]{:S(2)}) async-start(), calls=%async_computation.3 | async-start | bytes 327680
  208.4 26.8 %collective-permute-start.18 = (f32[3,4,128]{2,0,1:T(4,128)S(1)}, f32[3,4,128]{2,0,1:T(4,128)S(1)}, u32[]{:S(2)}, u32[]{:S(2)}) collective-permute-start(f32[3,4,128]{2,0,1:T(4,128)S(1)} %get-tuple-element.1748), channel_id=1, source_target_pairs={{0,4},{4,8},{8,12},{12,0},{1,5},{5,9},{9,13},{13,1},{2,6},{6,10},{... | collective-permute-start | bytes 18440 | tf_op jit(solution)/shard_map/ppermute | solution.py:16
Sparse Core Ops, SparseCore 0:
  208.5 26.7 reduce-scatter.6
  237.8 18.7 reduce-scatter.8
